TPU v7x, 128 devices: a whole 4x4x4 slice. The times are simulated.
128 devices in a mesh: req: 4 (over z), exp: 32 (over x, y, core).
Axes of the slice: x: 4, y: 4, z: 4, core: 2. Of those that a mesh axis runs over, the one named last changes fastest.
Arguments:
- queries: bfloat16 [128, 64, 2048], P(('req', 'exp'))
- new_kv: bfloat16 [128, 64, 2, 2048], P(('req', 'exp')), may hold values from -6 to 6
- cache: bfloat16 [128, 512, 2, 2048], P(('req', 'exp'))
- lengths: int32 [128], P(('req', 'exp')), may hold values from 8 to 448
- residual: bfloat16 [128, 64, 2048], P(('req', 'exp')), may hold values from -6 to 6
- out_weight: bfloat16 [2048, 2048], replicated, may hold values from -0.125 to 0.125
- norm_gain: float32 [2048], replicated, may hold values from 0.1 to 1.9
- expert_ids: int32 [128, 64, 8], P(('req', 'exp')), may hold values from 0 to 63, all different within a row; in each aligned block of 64 rows (0 to 63, 64 to 127, ..., all dimensions but the last counted through in order) at most 10 rows name the same one
- gates: float32 [128, 64, 8], P(('req', 'exp')), may hold values from 0.1 to 1
- w_gate: bfloat16 [128, 2048, 512], P(('req', 'exp')), may hold values from -0.125 to 0.125
- w_up: bfloat16 [128, 2048, 512], P(('req', 'exp')), may hold values from -0.125 to 0.125
- w_down: bfloat16 [128, 512, 2048], P(('req', 'exp')), may hold values from -0.1875 to 0.1875
Outputs:
- layer_out: bfloat16 [128, 64, 2048], P(('req', 'exp'))
- appended: bfloat16 [128, 512, 2, 2048], P(('req', 'exp'))
Inputs may be any that keep to these rules, and one draw needn't show every extreme that they name: `expert_ids`: among the tokens of one request, no expert is named by more than 10 rows.
All inputs are finite; a program needn't handle non-finite values.
Results may differ from a plain program's by a relative error of at most 0.0095.
Values may be sent and summed in bfloat16 or wider, within the bound.
A program may use at most 128 MiB of HBM per device.

v0:
```python
import jax
import jax.numpy as jnp
from jax import lax
from jax.sharding import PartitionSpec as P

HEADS = 16
HEAD_DIM = 128


masked_value = -1e30


def expert_rows(piece, gate_half, up_half, down_half):
    leading, counted, features = piece.shape
    flat_rows = piece.reshape(leading * counted, features)
    gate_act = jnp.dot(flat_rows, gate_half, preferred_element_type=jnp.float32)
    upward = jnp.dot(flat_rows, up_half, preferred_element_type=jnp.float32)
    hidden = (jax.nn.silu(gate_act) * upward).astype(jnp.bfloat16)
    partial_sum = jnp.dot(hidden, down_half, preferred_element_type=jnp.float32)
    return partial_sum.reshape(leading, counted, partial_sum.shape[-1])


def shards(
    queries,
    new_kv,
    cache,
    lengths,
    residual,
    out_weight,
    norm_gain,
    expert_ids,
    gates,
    w_gate,
    w_up,
    w_down,
):
    gate_half = w_gate[0]
    up_half = w_up[0]
    down_half = w_down[0]
    query_rows = queries[0]
    new_rows = new_kv[0]
    cache_rows = cache[0]
    length_now = lengths[0]
    group_len = query_rows.shape[0]
    features = query_rows.shape[1]
    key_rows = jnp.concatenate([cache_rows[:, 0], new_rows[:, 0]], axis=0)
    value_rows = jnp.concatenate([cache_rows[:, 1], new_rows[:, 1]], axis=0)
    positions = key_rows.shape[0]
    queried = query_rows.reshape(group_len, HEADS, HEAD_DIM)
    keyed = key_rows.reshape(positions, HEADS, HEAD_DIM)
    valued = value_rows.reshape(positions, HEADS, HEAD_DIM)
    scores = jnp.einsum(
        "qhd,khd->hqk", queried, keyed, preferred_element_type=jnp.float32
    ) * HEAD_DIM ** (-0.5)
    slot_place = jnp.arange(positions, dtype=jnp.int32)
    counted = (slot_place < length_now) | (slot_place >= cache_rows.shape[0])
    scores = jnp.where(counted[None, None, :], scores, masked_value)
    peak_score = jnp.max(scores, axis=-1, keepdims=True)
    raised = jnp.exp(scores - peak_score)
    softmax_bf = (raised / jnp.sum(raised, axis=-1, keepdims=True)).astype(jnp.bfloat16)
    mixed_heads = jnp.einsum("hqk,khd->qhd", softmax_bf, valued, preferred_element_type=jnp.float32)
    attention = mixed_heads.reshape(group_len, features).astype(jnp.bfloat16)
    stream = residual[0].astype(jnp.float32) + jnp.dot(
        attention, out_weight, preferred_element_type=jnp.float32
    )
    appended = lax.dynamic_update_slice(
        cache_rows, new_rows, (length_now, jnp.int32(0), jnp.int32(0))
    )[None]
    mean_square = jnp.mean(stream * stream, axis=-1, keepdims=True)
    normed = (stream * lax.rsqrt(mean_square + 1e-06) * norm_gain).astype(jnp.bfloat16)
    devices_all = lax.axis_size(("req", "exp"))
    experts_all = devices_all // 2
    top_k = expert_ids.shape[2]
    capacity = 5 * group_len * top_k // (4 * experts_all)
    routed = expert_ids[0].reshape(-1)
    one_hot = (routed[:, None] == jnp.arange(experts_all, dtype=jnp.int32)[None, :]).astype(
        jnp.int32
    )
    ranking = jnp.sum((jnp.cumsum(one_hot, axis=0) - one_hot) * one_hot, axis=1)
    position = routed * capacity + ranking
    row_token = jnp.arange(group_len * top_k, dtype=jnp.int32) // top_k
    token_of = jnp.full((experts_all * capacity,), group_len, jnp.int32).at[position].set(row_token)
    padded = jnp.concatenate([normed, jnp.zeros((1, features), jnp.bfloat16)], axis=0)
    outgoing = padded[token_of].reshape(experts_all, capacity, features)
    doubled = jnp.broadcast_to(outgoing[:, None], (experts_all, 2, capacity, features)).reshape(
        devices_all, capacity, features
    )
    partials = expert_rows(
        lax.all_to_all(doubled, ("req", "exp"), split_axis=0, concat_axis=0, tiled=True),
        gate_half,
        up_half,
        down_half,
    )
    returned = lax.all_to_all(
        partials.astype(jnp.bfloat16), ("req", "exp"), split_axis=0, concat_axis=0, tiled=True
    ).astype(partials.dtype)
    expert_out = jnp.sum(returned.reshape(experts_all, 2, capacity, features), axis=1).astype(
        jnp.bfloat16
    )
    picked = expert_out.reshape(experts_all * capacity, features)[position].reshape(
        group_len, top_k, features
    )
    blended = jnp.sum(gates[0][:, :, None] * picked.astype(jnp.float32), axis=1)
    layer_out = (stream + blended).astype(jnp.bfloat16)[None]
    return (layer_out, appended)


def solution(mesh):
    placed = (
        P(("req", "exp"), None, None),
        P(("req", "exp"), None, None, None),
        P(("req", "exp"), None, None, None),
        P(("req", "exp")),
        P(("req", "exp"), None, None),
        P(),
        P(),
        P(("req", "exp"), None, None),
        P(("req", "exp"), None, None),
        P(("req", "exp"), None, None),
        P(("req", "exp"), None, None),
        P(("req", "exp"), None, None),
    )
    return jax.shard_map(
        shards,
        mesh=mesh,
        in_specs=placed,
        out_specs=(P(("req", "exp"), None, None), P(("req", "exp"), None, None, None)),
        check_vma=False,
    )
```

profile of v0, /device:TPU:2, one launch (start us, length us, event | category | flops | bytes accessed | tf_op | source)
XLA Modules:
  0.0 340.7 jit_solution(17939596780103272236)
XLA Ops:
  0.7 7.2 %copy.68 = bf16[1,512,2,2048]{3,2,1,0:T(2,128)(2,1)} copy(bf16[1,512,2,2048]{3,2,1,0:T(2,128)(2,1)} %param.14) | data formatting | bytes 8388608
  8.2 11.1 %copy.30 = bf16[1,512,2,2048]{1,3,2,0:T(8,128)(2,1)} copy(bf16[1,512,2,2048]{3,2,1,0:T(2,128)(2,1)} %copy.68) | data formatting | bytes 8388608 | tf_op args[2]
  19.3 4.5 %fusion.47 = (bf16[512,1,2048]{0,2,1:T(8,128)(2,1)}, bf16[512,1,2048]{0,2,1:T(8,128)(2,1)}) fusion(bf16[512,2,2048]{0,2,1:T(8,128)(2,1)} %bitcast.90), kind=kLoop, calls=%fused_computation.78 | loop fusion | bytes 8388608 | tf_op jit(solution)/shard_map/slice | solution.py:46
  23.8 4.0 %copy.33 = bf16[512,16,128]{2,0,1:T(8,128)(2,1)} copy(bf16[512,16,128]{0,2,1:T(8,128)(2,1)} %bitcast.92) | data formatting | bytes 4194304 | tf_op jit(solution)/shard_map/concatenate | solution.py:46
  27.8 2.3 slice_reduce_fusion.1
  31.8 3.9 %copy.31 = bf16[512,16,128]{2,0,1:T(8,128)(2,1)} copy(bf16[512,16,128]{0,2,1:T(8,128)(2,1)} %bitcast.91) | data formatting | bytes 4194304 | tf_op jit(solution)/shard_map/concatenate | solution.py:47
  35.8 2.7 fusion.5
  45.8 2.6 scatter_custom_fusion
  48.6 4.1 %gather_fusion = bf16[640,2048]{1,0:T(8,128)(2,1)} fusion(bf16[65,2048]{1,0:T(8,128)(2,1)S(1)} %concatenate.25, s32[1024]{0:T(1024)S(1)} %pad_clamp_fusion.1), kind=kCustom, calls=%fused_computation | custom fusion | bytes 5245440 | tf_op jit(solution)/shard_map/gather | solution.py:84
  52.7 5.4 %broadcast_in_dim.42 = bf16[64,10,2048]{2,1,0:T(8,128)(2,1)} reshape(bf16[640,2048]{1,0:T(8,128)(2,1)} %gather_fusion) | data formatting | bytes 5242880 | tf_op jit(solution)/shard_map/broadcast_in_dim | solution.py:85
  58.0 6.8 %broadcast_in_dim.43 = bf16[64,2,10,2048]{3,2,1,0:T(8,128)(2,1)} broadcast(bf16[64,10,2048]{2,1,0:T(8,128)(2,1)} %broadcast_in_dim.42), dimensions={0,2,3} | broadcast | bytes 7864320 | tf_op jit(solution)/shard_map/broadcast_in_dim | solution.py:85
  64.8 108.1 %all_to_all.10 = bf16[128,10,2048]{2,1,0:T(8,128)(2,1)} all-to-all(bf16[128,10,2048]{2,1,0:T(8,128)(2,1)} %bitcast.87), channel_id=1, replica_groups=mesh['req'=4,'exp'=32] {'req','exp'}, dimensions={0} | all-to-all | bytes 10485760 | tf_op jit(solution)/shard_map/all_to_all | solution.py:89
  172.9 9.8 %reshape.109 = bf16[1280,2048]{1,0:T(8,128)(2,1)} reshape(bf16[128,10,2048]{2,1,0:T(8,128)(2,1)} %all_to_all.10) | data formatting | bytes 10485760 | tf_op jit(solution)/shard_map/reshape | solution.py:15
  182.7 5.6 %fusion.15 = f32[1280,512]{1,0:T(8,128)S(1)} fusion(bf16[1280,2048]{1,0:T(8,128)(2,1)} %reshape.109, bf16[1,2048,512]{2,1,0:T(8,128)(2,1)} %param.21), kind=kOutput, calls=%fused_computation.27 | convolution fusion | flops 2684354560 | bytes 9961472 | tf_op jit(solution)/shard_map/dot_general | solution.py:16
  188.3 4.4 %fusion.2 = bf16[1280,512]{1,0:T(8,128)(2,1)} fusion(bf16[1280,2048]{1,0:T(8,128)(2,1)S(1)} %copy-done.1, f32[1280,512]{1,0:T(8,128)S(1)} %fusion.15, bf16[1,2048,512]{2,1,0:T(8,128)(2,1)S(1)} %copy-done.8), kind=kOutput, calls=%fused_computation.9 | convolution fusion | flops 2688286720 | bytes 11272192 | tf_op jit(solution)/shard_map/dot_general | solution.py:17
  192.7 3.6 %dot_general.25 = bf16[128,10,512]{2,1,0:T(8,128)(2,1)} reshape(bf16[1280,512]{1,0:T(8,128)(2,1)} %fusion.2) | data formatting | bytes 2621440 | tf_op jit(solution)/shard_map/dot_general | solution.py:19
  196.3 6.4 %convolution_convert_fusion = bf16[128,10,2048]{2,0,1:T(8,128)(2,1)S(1)} fusion(bf16[1,512,2048]{2,1,0:T(8,128)(2,1)S(1)} %copy-done, bf16[128,10,512]{2,1,0:T(8,128)(2,1)} %dot_general.25), kind=kOutput, calls=%fused_computation.7 | convolution fusion | flops 2686976000 | bytes 8650752 | tf_op jit(solution)/shard_map/dot_general | solution.py:19
  202.7 6.5 %copy.43 = bf16[128,10,2048]{2,1,0:T(8,128)(2,1)} copy(bf16[128,10,2048]{2,0,1:T(8,128)(2,1)S(1)} %convolution_convert_fusion) | data formatting | bytes 10485760 | tf_op jit(solution)/shard_map/convert_element_type | solution.py:95
  209.3 6.3 %all-to-all-start.1 = ((bf16[128,10,2048]{2,1,0:T(8,128)(2,1)}), bf16[128,10,2048]{2,1,0:T(8,128)(2,1)}, u32[]{:S(2)}, u32[]{:S(2)}) async-start(bf16[128,10,2048]{2,1,0:T(8,128)(2,1)} %copy.43), calls=%async_computation.1 | async-start | bytes 16777216 | tf_op jit(solution)/shard_map/all_to_all | solution.py:94
  216.8 97.9 %all-to-all-done.1 = bf16[128,10,2048]{2,1,0:T(8,128)(2,1)} async-done(((bf16[128,10,2048]{2,1,0:T(8,128)(2,1)}), bf16[128,10,2048]{2,1,0:T(8,128)(2,1)}, u32[]{:S(2)}, u32[]{:S(2)}) %all-to-all-start.1) | async-done | bytes 5242912 | tf_op jit(solution)/shard_map/all_to_all | solution.py:94
  314.7 9.0 %bitcast_reduce_fusion = bf16[64,10,2048]{2,1,0:T(8,128)(2,1)} fusion(bf16[128,10,2048]{2,1,0:T(8,128)(2,1)} %all-to-all-done.1), kind=kLoop, calls=%fused_computation.4 | loop fusion | flops 1310720 | bytes 7864320 | tf_op jit(solution)/shard_map/reduce_sum | solution.py:97
  323.7 5.5 %convert_element_type.63 = bf16[640,2048]{1,0:T(8,128)(2,1)} reshape(bf16[64,10,2048]{2,1,0:T(8,128)(2,1)} %bitcast_reduce_fusion) | data formatting | bytes 5242880 | tf_op jit(solution)/shard_map/convert_element_type | solution.py:97
  329.2 7.3 %gather_fusion.1 = bf16[512,2048]{1,0:T(8,128)(2,1)} fusion(bf16[640,2048]{1,0:T(8,128)(2,1)} %convert_element_type.63, s32[1024]{0:T(1024)S(1)} %pad_clamp_fusion), kind=kCustom, calls=%fused_computation.1 | custom fusion | bytes 4196352 | tf_op jit(solution)/shard_map/gather | solution.py:100
  336.5 3.4 %fusion.1 = f32[64,2048]{1,0:T(8,128)S(1)} fusion(bf16[512,2048]{1,0:T(8,128)(2,1)} %gather_fusion.1, f32[64,8]{1,0:T(8,128)S(1)} %copy.37), kind=kLoop, calls=%fused_computation.6 | loop fusion | flops 3014656 | bytes 2623488 | tf_op jit(solution)/shard_map/reduce_sum | solution.py:103
  (53 shorter events, 10.8 us)
Async XLA Ops:
  0.6 195.7 %copy-start = (bf16[1,512,2048]{2,1,0:T(8,128)(2,1)S(1)}, bf16[1,512,2048]{2,1,0:T(8,128)(2,1)}, u32[]{:S(2)}) copy-start(bf16[1,512,2048]{2,1,0:T(8,128)(2,1)} %param.23) | copy-start | bytes 6291460
  0.6 7.2 %copy-start.5 = (s32[1,64,8]{1,2,0:T(8,128)S(1)}, s32[1,64,8]{1,2,0:T(8,128)}, u32[]{:S(2)}) copy-start(s32[1,64,8]{1,2,0:T(8,128)} %param.19) | copy-start | bytes 6148
  23.8 4.0 %copy-start.2 = (bf16[1,64,2,2048]{3,2,1,0:T(2,128)(2,1)S(1)}, bf16[1,64,2,2048]{3,2,1,0:T(2,128)(2,1)}, u32[]{:S(2)}) copy-start(bf16[1,64,2,2048]{3,2,1,0:T(2,128)(2,1)} %param.13) | copy-start | bytes 1572868
  35.8 3.7 %copy-start.3 = (bf16[512,16,128]{2,0,1:T(8,128)(2,1)S(1)}, bf16[512,16,128]{2,0,1:T(8,128)(2,1)}, u32[]{:S(2)}) copy-start(bf16[512,16,128]{2,0,1:T(8,128)(2,1)} %copy.31) | copy-start | bytes 6291460
  38.4 2.2 slice-start
  39.4 2.8 slice-start.1
  39.4 2.8 copy-start.4
  42.2 6.2 %copy-start.6 = (f32[2048]{0:T(1024)S(1)}, f32[2048]{0:T(1024)}, u32[]{:S(2)}) copy-start(f32[2048]{0:T(1024)} %param.18) | copy-start | bytes 24580
  182.7 5.6 %copy-start.1 = (bf16[1280,2048]{1,0:T(8,128)(2,1)S(1)}, bf16[1280,2048]{1,0:T(8,128)(2,1)}, u32[]{:S(2)}) copy-start(bf16[1280,2048]{1,0:T(8,128)(2,1)} %reshape.109) | copy-start | bytes 15728644
  182.7 5.6 %copy-start.8 = (bf16[1,2048,512]{2,1,0:T(8,128)(2,1)S(1)}, bf16[1,2048,512]{2,1,0:T(8,128)(2,1)}, u32[]{:S(2)}) copy-start(bf16[1,2048,512]{2,1,0:T(8,128)(2,1)} %param.22) | copy-start | bytes 6291460
  209.3 6.3 %copy-start.7 = (f32[1,64,8]{1,2,0:T(8,128)S(1)}, f32[1,64,8]{1,2,0:T(8,128)}, u32[]{:S(2)}) copy-start(f32[1,64,8]{1,2,0:T(8,128)} %param.20) | copy-start | bytes 6148
  209.3 105.4 %all-to-all-start.1 = ((bf16[128,10,2048]{2,1,0:T(8,128)(2,1)}), bf16[128,10,2048]{2,1,0:T(8,128)(2,1)}, u32[]{:S(2)}, u32[]{:S(2)}) async-start(bf16[128,10,2048]{2,1,0:T(8,128)(2,1)} %copy.43), calls=%async_computation.1 | async-start | bytes 16777216 | tf_op jit(solution)/shard_map/all_to_all | solution.py:94
where the time goes:
time: 343 us; the launch traced here: 341 us
  blocking collectives  108 us (31%)
  waiting for transfers between devices  97.9 us (29%)
  local copies, waits for them, and re-layouts  89.9 us (26%)
  matrix products  21.4 us (6%)
  other arithmetic  15.7 us (5%)
  starting transfers between devices  6.3 us (2%)
    all_to_all x1, blocking collectives, shards(): lax.all_to_all(doubled, ('req', 'exp'), split_axis=0, concat_axis=0, tile...  108 us
    all_to_all x1, waiting for transfers between devices, shards(): lax.all_to_all(partials.astype(jnp.bfloat16), ('req', 'exp'), split_axis=...  97.9 us
    unnamed x26, local copies, waits for them, and re-layouts  21.6 us
    broadcast_in_dim x2, local copies, waits for them, and re-layouts, shards(): jnp.broadcast_to(outgoing[:, None], (experts_all, 2, capacity, features))  12.1 us
    reshape x1, local copies, waits for them, and re-layouts, expert_rows(): flat_rows = piece.reshape(leading * counted, features)  9.85 us
    reduce_sum x1, other arithmetic, shards(): jnp.sum(returned.reshape(experts_all, 2, capacity, features), axis=1)  9 us
    gather x1, local copies, waits for them, and re-layouts, shards(): expert_out.reshape(experts_all * capacity, features)[position]  7.29 us
  transfers between devices with their start and end apart: 1, of which 1 were waited for; matrix products, arithmetic and copies ran while one was open for 0% of the time, Pallas kernels for 0%

commit v1 on v0

v1 whole, which is shorter than its diff:
```python
import functools

import jax
import jax.numpy as jnp
from jax import lax
from jax.experimental import pallas as pl
from jax.experimental.pallas import tpu as pltpu
from jax.sharding import PartitionSpec as P

MESH = pl.DeviceIdType.MESH
F32 = jnp.float32
BF16 = jnp.bfloat16

GROUP = 64
D = 2048
HEADS = 16
HEAD_DIM = 128
EXPERTS = 64
TOP = 8
HALF = 512
CAP = 10
CACHE = 512
SEEN = 448
LANES = 128
PIECES = D // LANES
CHUNKS = 4
PEERS = EXPERTS // CHUNKS
ROWS = PEERS * CAP
MASKED = -1e30


def dot(a, b, dims=((1,), (0,))):
    return lax.dot_general(a, b, (dims, ((), ())), preferred_element_type=F32)


def offsets(i):
    dx, dy = (i // 4) % 4, i % 4
    return (i // PEERS + 8 - dx - dy) % 4, dx, dy


def layer_kernel(
    length_ref,
    ids_ref,
    gates_ref,
    gain_ref,
    q_hbm,
    kv_hbm,
    cache_hbm,
    res_hbm,
    ow_hbm,
    wg_hbm,
    wu_hbm,
    wd_hbm,
    out_ref,
    q_ref,
    kv_ref,
    res_ref,
    ow_ref,
    wg_ref,
    wu_ref,
    wd_ref,
    att_ref,
    stream_ref,
    normed_ref,
    pick_ref,
    mixhi_ref,
    mixlo_ref,
    wide_ref,
    x_ref,
    h_ref,
    out_rows,
    in_rows,
    done_rows,
    back_rows,
    local_sem,
    mate_send,
    mate_recv,
    send_sem,
    recv_sem,
    back_send,
    back_recv,
):
    z = lax.axis_index("req")
    along = lax.axis_index("exp")
    core = along % 2
    x = along // 8
    y = (along // 2) % 4

    def device(i, sign):
        dz, dx, dy = offsets(i)
        there = (((x + sign * dx + 4) % 4) * 4 + (y + sign * dy + 4) % 4) * 2 + core
        return {"req": (z + sign * dz + 4) % 4, "exp": there}

    mate = {"req": z, "exp": along + 1 - 2 * core}

    barrier = pltpu.get_barrier_semaphore()

    def greet(i, carry):
        pl.semaphore_signal(barrier, inc=1, device_id=device(i, 1), device_id_type=MESH)
        return carry

    lax.fori_loop(1, EXPERTS, greet, 0)
    pl.semaphore_signal(barrier, inc=1, device_id=mate, device_id_type=MESH)

    loads = [
        pltpu.make_async_copy(cache_hbm.at[pl.ds(0, SEEN)], kv_ref.at[pl.ds(0, SEEN)], local_sem.at[0]),
        pltpu.make_async_copy(kv_hbm, kv_ref.at[pl.ds(SEEN, GROUP)], local_sem.at[1]),
        pltpu.make_async_copy(q_hbm, q_ref, local_sem.at[2]),
        pltpu.make_async_copy(res_hbm, res_ref, local_sem.at[3]),
        pltpu.make_async_copy(ow_hbm, ow_ref, local_sem.at[4]),
        pltpu.make_async_copy(wg_hbm, wg_ref.at[core], local_sem.at[5]),
        pltpu.make_async_copy(wu_hbm, wu_ref.at[core], local_sem.at[6]),
        pltpu.make_async_copy(wd_hbm, wd_ref.at[core], local_sem.at[7]),
    ]
    for copy in (loads[2], loads[1], loads[0], loads[3], loads[4]):
        copy.start()
    for copy in loads[5:]:
        copy.start()
    swaps = [
        pltpu.make_async_remote_copy(
            src_ref=src, dst_ref=dst.at[core], send_sem=mate_send.at[k], recv_sem=mate_recv.at[k],
            device_id=mate, device_id_type=MESH,
        )
        for k, (src, dst) in enumerate(((wg_hbm, wg_ref), (wu_hbm, wu_ref), (wd_hbm, wd_ref)))
    ]

    expert_of = lax.broadcasted_iota(jnp.int32, (EXPERTS, GROUP), 0)
    hit = jnp.zeros((EXPERTS, GROUP), F32)
    gate_of = jnp.zeros((EXPERTS, GROUP), F32)
    for k in range(TOP):
        same = ids_ref[k : k + 1, :] == expert_of
        hit = jnp.where(same, 1.0, hit)
        gate_of = jnp.where(same, gates_ref[k : k + 1, :], gate_of)
    t_row = lax.broadcasted_iota(jnp.int32, (GROUP, GROUP), 0)
    t_col = lax.broadcasted_iota(jnp.int32, (GROUP, GROUP), 1)
    before = jnp.where(t_row < t_col, 1.0, 0.0).astype(BF16)
    eye = jnp.where(t_row == t_col, 1.0, 0.0).astype(BF16)
    rank = dot(hit.astype(BF16), before)
    rank = jnp.where(hit > 0.5, rank, 99.0).astype(BF16)
    gate_hi = gate_of.astype(BF16)
    gate_lo = (gate_of - gate_hi.astype(F32)).astype(BF16)

    def slots(shape, axis):
        row = lax.broadcasted_iota(jnp.int32, shape, axis)
        i = (row * 6554) >> 16
        dx, dy = (i >> 2) & 3, i & 3
        dz = ((i >> 4) + 8 - dx - dy) & 3
        expert = (((z + dz) & 3) << 4) + (((x + dx) & 3) << 2) + ((y + dy) & 3)
        return (row - i * CAP).astype(F32), expert

    slot, expert = slots((EXPERTS * CAP, EXPERTS), 0)
    spread = jnp.where(expert == lax.broadcasted_iota(jnp.int32, expert.shape, 1), 1.0, 0.0).astype(BF16)
    pick_ref[...] = jnp.where(dot(spread, rank) == slot, 1.0, 0.0).astype(BF16)
    slot, expert = slots((EXPERTS, EXPERTS * CAP), 1)
    spread = jnp.where(expert == lax.broadcasted_iota(jnp.int32, expert.shape, 0), 1.0, 0.0).astype(BF16)
    turned = ((1,), (1,))
    chosen = dot(dot(eye, rank, turned).astype(BF16), spread) == slot
    for table, part in ((mixhi_ref, gate_hi), (mixlo_ref, gate_lo)):
        spread_gate = dot(dot(eye, part, turned).astype(BF16), spread)
        whole = jnp.where(chosen, spread_gate, 0.0).astype(BF16)
        for j in range(CHUNKS):
            table[j] = whole[:, j * ROWS : (j + 1) * ROWS]

    for copy in (loads[2], loads[1], loads[0]):
        copy.wait()
    column = lax.broadcasted_iota(jnp.int32, (GROUP, 2 * (SEEN + GROUP)), 1)
    place = column >> 1
    length = length_ref[0]
    counted = ((column & 1) == 0) & ((place < length) | (place >= SEEN))

    def head(h, carry):
        at = pl.ds(pl.multiple_of(h * HEAD_DIM, HEAD_DIM), HEAD_DIM)
        pairs = kv_ref[:, :, at].reshape(2 * (SEEN + GROUP), HEAD_DIM)
        scores = dot(q_ref[:, at], pairs, ((1,), (1,))) * HEAD_DIM ** (-0.5)
        scores = jnp.where(counted, scores, MASKED)
        raised = jnp.exp(scores - jnp.max(scores, axis=1, keepdims=True))
        share = raised / jnp.sum(raised, axis=1, keepdims=True)
        share = pltpu.roll(share, 1, 1).astype(BF16)
        att_ref[:, at] = dot(share, pairs).astype(BF16)
        return carry

    lax.fori_loop(0, HEADS // 2, head, 0)
    pl.semaphore_wait(barrier, EXPERTS)
    for swap in swaps:
        swap.start()
    lax.fori_loop(HEADS // 2, HEADS, head, 0)

    for copy in loads[3:5]:
        copy.wait()

    def project(n, carry):
        at = pl.ds(pl.multiple_of(n * 256, 256), 256)
        stream_ref[:, at] = res_ref[:, at].astype(F32) + dot(att_ref[...], ow_ref[:, at])
        return carry

    lax.fori_loop(0, D // 256, project, 0)
    stream = stream_ref[...]
    mean_square = jnp.mean(stream * stream, axis=1, keepdims=True)
    normed_ref[...] = (stream * lax.rsqrt(mean_square + 1e-06) * gain_ref[...]).astype(BF16)

    def send_copy(i):
        return pltpu.make_async_remote_copy(
            src_ref=out_rows.at[i], dst_ref=in_rows.at[i], send_sem=send_sem.at[i], recv_sem=recv_sem.at[i],
            device_id=device(i, 1), device_id_type=MESH,
        )

    def back_copy(i):
        return pltpu.make_async_remote_copy(
            src_ref=done_rows.at[i], dst_ref=back_rows.at[i], send_sem=back_send.at[i], recv_sem=back_recv.at[i],
            device_id=device(i, -1), device_id_type=MESH,
        )

    own_out = pltpu.make_async_copy(out_rows.at[0], in_rows.at[0], recv_sem.at[0])
    own_back = pltpu.make_async_copy(done_rows.at[0], back_rows.at[0], back_recv.at[0])

    def tiles_out(rows, j):
        rows[pl.ds(j * PEERS, PEERS)] = wide_ref[...].reshape(PEERS, CAP, PIECES, LANES).astype(BF16)

    def tiles_in(rows, j):
        wide_ref[...] = rows[pl.ds(j * PEERS, PEERS)].astype(F32).reshape(ROWS * PIECES, LANES)
        for c in range(PIECES):
            x_ref[:, c * LANES : (c + 1) * LANES] = wide_ref[pl.ds(c, ROWS, stride=PIECES), :].astype(BF16)

    def each_peer(j, action):
        def body(i, carry):
            action(i)
            return carry

        lax.fori_loop(j * PEERS + (1 if j == 0 else 0), (j + 1) * PEERS, body, 0)

    for j in range(CHUNKS):
        picked = pick_ref[j * ROWS : (j + 1) * ROWS, :]
        for c in range(PIECES):
            wide_ref[pl.ds(c, ROWS, stride=PIECES), :] = dot(picked, normed_ref[:, c * LANES : (c + 1) * LANES])
        tiles_out(out_rows, j)
        if j == 0:
            own_out.start()
        each_peer(j, lambda i: send_copy(i).start())

    for copy in loads[5:]:
        copy.wait()
    for swap in swaps:
        swap.wait()

    for j in range(CHUNKS):
        if j == 0:
            own_out.wait()
        each_peer(j, lambda i: send_copy(i).wait_recv())
        tiles_in(in_rows, j)

        def hidden(n, carry):
            half, at = n // 2, pl.ds(pl.multiple_of((n % 2) * 256, 256), 256)
            gate = dot(x_ref[...], wg_ref[half, :, at])
            up = dot(x_ref[...], wu_ref[half, :, at])
            h_ref[:, pl.ds(pl.multiple_of(n * 256, 256), 256)] = (gate / (1.0 + jnp.exp(-gate)) * up).astype(BF16)
            return carry

        lax.fori_loop(0, 4, hidden, 0)

        def down(n, carry):
            at = pl.ds(pl.multiple_of(n * 256, 256), 256)
            rows = dot(h_ref[:, :HALF], wd_ref[0, :, at]) + dot(h_ref[:, HALF:], wd_ref[1, :, at])
            wide_ref[pl.ds(2 * n, ROWS, stride=PIECES), :] = rows[:, :LANES]
            wide_ref[pl.ds(2 * n + 1, ROWS, stride=PIECES), :] = rows[:, LANES:]
            return carry

        lax.fori_loop(0, D // 256, down, 0)
        tiles_out(done_rows, j)
        if j == 0:
            own_back.start()
        each_peer(j, lambda i: back_copy(i).start())

    for j in range(CHUNKS):
        if j == 0:
            own_back.wait()
        each_peer(j, lambda i: back_copy(i).wait_recv())
        tiles_in(back_rows, j)
        for n in range(D // 512):
            at = slice(n * 512, (n + 1) * 512)
            stream_ref[:, at] += dot(mixhi_ref[j], x_ref[:, at]) + dot(mixlo_ref[j], x_ref[:, at])
    out_ref[...] = stream_ref[...].astype(BF16)

    for j in range(CHUNKS):
        each_peer(j, lambda i: send_copy(i).wait_send())
        each_peer(j, lambda i: back_copy(i).wait_send())


def append_kernel(length_ref, kv_hbm, cache_hbm, out_hbm, held, new, in_sem, out_sem):
    pieces = 8
    size = CACHE // pieces
    parts = [pl.ds(k * size, size) for k in range(pieces)]
    ins = [pltpu.make_async_copy(cache_hbm.at[p], held.at[p], in_sem.at[k]) for k, p in enumerate(parts)]
    outs = [pltpu.make_async_copy(held.at[p], out_hbm.at[p], out_sem.at[k]) for k, p in enumerate(parts)]
    fetch = pltpu.make_async_copy(kv_hbm, new, in_sem.at[pieces])
    for copy in ins:
        copy.start()
    fetch.start()
    for arrive, leave in zip(ins, outs):
        arrive.wait()
        leave.start()
    fetch.wait()
    for leave in outs:
        leave.wait()
    write = pltpu.make_async_copy(new, out_hbm.at[pl.ds(length_ref[0], GROUP)], out_sem.at[pieces])
    write.start()
    write.wait()


def shards(
    queries, new_kv, cache, lengths, residual, out_weight, norm_gain, expert_ids, gates, w_gate, w_up, w_down
):
    anywhere = pl.BlockSpec(memory_space=pl.ANY)
    in_vmem = pl.BlockSpec(memory_space=pltpu.VMEM)
    in_smem = pl.BlockSpec(memory_space=pltpu.SMEM)
    tiles = (EXPERTS, CAP, PIECES, LANES)
    layer_out = pl.pallas_call(
        layer_kernel,
        name="layer",
        out_shape=jax.ShapeDtypeStruct((GROUP, D), BF16),
        in_specs=[in_smem, in_vmem, in_vmem, in_vmem] + [anywhere] * 8,
        out_specs=in_vmem,
        scratch_shapes=[
            pltpu.VMEM((GROUP, D), BF16),
            pltpu.VMEM((SEEN + GROUP, 2, D), BF16),
            pltpu.VMEM((GROUP, D), BF16),
            pltpu.VMEM((D, D), BF16),
            pltpu.VMEM((2, D, HALF), BF16),
            pltpu.VMEM((2, D, HALF), BF16),
            pltpu.VMEM((2, HALF, D), BF16),
            pltpu.VMEM((GROUP, D), BF16),
            pltpu.VMEM((GROUP, D), F32),
            pltpu.VMEM((GROUP, D), BF16),
            pltpu.VMEM((EXPERTS * CAP, GROUP), BF16),
            pltpu.VMEM((CHUNKS, GROUP, ROWS), BF16),
            pltpu.VMEM((CHUNKS, GROUP, ROWS), BF16),
            pltpu.VMEM((ROWS * PIECES, LANES), F32),
            pltpu.VMEM((ROWS, D), BF16),
            pltpu.VMEM((ROWS, 2 * HALF), BF16),
            pltpu.VMEM(tiles, BF16),
            pltpu.VMEM(tiles, BF16),
            pltpu.VMEM(tiles, BF16),
            pltpu.VMEM(tiles, BF16),
            pltpu.SemaphoreType.DMA((8,)),
            pltpu.SemaphoreType.DMA((3,)),
            pltpu.SemaphoreType.DMA((3,)),
            pltpu.SemaphoreType.DMA((EXPERTS,)),
            pltpu.SemaphoreType.DMA((EXPERTS,)),
            pltpu.SemaphoreType.DMA((EXPERTS,)),
            pltpu.SemaphoreType.DMA((EXPERTS,)),
        ],
        compiler_params=pltpu.CompilerParams(
            collective_id=0, has_side_effects=True, vmem_limit_bytes=60 * 1024 * 1024
        ),
    )(
        lengths,
        expert_ids[0].T,
        gates[0].T,
        norm_gain[None],
        queries[0],
        new_kv[0],
        cache[0],
        residual[0],
        out_weight,
        w_gate[0],
        w_up[0],
        w_down[0],
    )
    appended = pl.pallas_call(
        append_kernel,
        name="append",
        out_shape=jax.ShapeDtypeStruct((CACHE, 2, D), BF16),
        in_specs=[in_smem, anywhere, anywhere],
        out_specs=anywhere,
        scratch_shapes=[
            pltpu.VMEM((CACHE, 2, D), BF16),
            pltpu.VMEM((GROUP, 2, D), BF16),
            pltpu.SemaphoreType.DMA((9,)),
            pltpu.SemaphoreType.DMA((9,)),
        ],
    )(lengths, new_kv[0], cache[0])
    return layer_out[None], appended[None]


def solution(mesh):
    shared = ("req", "exp")
    three, four = P(shared, None, None), P(shared, None, None, None)
    return jax.shard_map(
        shards,
        mesh=mesh,
        in_specs=(three, four, four, P(shared), three, P(), P(), three, three, three, three, three),
        out_specs=(three, four),
        check_vma=False,
    )
```

time: 343 us -> 103 us (0.30)
  blocking collectives: 108 us -> 0 us
  Pallas kernels: 0 us -> 99.6 us
  waiting for transfers between devices: 97.9 us -> 0 us
  local copies, waits for them, and re-layouts: 89.9 us -> 0.71 us
  matrix products: 21.4 us -> 0 us
  other arithmetic: 15.7 us -> 0 us
  starting transfers between devices: 6.3 us -> 0 us
    all_to_all x1 -> x0, blocking collectives: 108 us -> none  [shards(): lax.all_to_all(doubled, ('req', 'exp'), split_axis=0, concat_axis=0, tile...]
    pallas_call x0 -> x2, Pallas kernels: none -> 99.6 us  [the longest x1 95.2 us: shards(): pl.pallas_call(layer_kernel, name='layer', out_shape=jax.ShapeDtypeStruct...]
    all_to_all x1 -> x0, waiting for transfers between devices: 97.9 us -> none  [shards(): lax.all_to_all(partials.astype(jnp.bfloat16), ('req', 'exp'), split_axis=...]
    dot_general x6 -> x0, matrix products: 21.4 us -> none  [the longest x1 6.42 us: expert_rows(): partial_sum = jnp.dot(hidden, down_half, preferred_element_type=jnp.float32)]
    unnamed x26 -> x3, local copies, waits for them, and re-layouts: 21.6 us -> 0.71 us
    reduce_sum x3 -> x0, other arithmetic: 12.5 us -> none  [the longest x1 9 us: shards(): jnp.sum(returned.reshape(experts_all, 2, capacity, features), axis=1)]
    broadcast_in_dim x2 -> x0, local copies, waits for them, and re-layouts: 12.1 us -> none  [shards(): jnp.broadcast_to(outgoing[:, None], (experts_all, 2, capacity, features))]
    convert_element_type x2 -> x0, local copies, waits for them, and re-layouts: 12 us -> none  [the longest x1 6.52 us: shards(): partials.astype(jnp.bfloat16)]
  transfers between devices with their start and end apart: 1 -> 0, of which waited for: 1 -> 0; matrix products, arithmetic and copies ran while one was open for 0% -> 0% of each run, Pallas kernels for 0% -> 0%
where the time goes in v1:
time: 103 us; the launch traced here: 102 us
  Pallas kernels  99.6 us (97%)
  between operations  1.31 us (1%)
    pallas_call x1, Pallas kernels, shards(): pl.pallas_call(layer_kernel, name='layer', out_shape=jax.ShapeDtypeStruct...  95.2 us
    pallas_call x1, Pallas kernels, shards(): pl.pallas_call(append_kernel, name='append', out_shape=jax.ShapeDtypeStru...  4.43 us

profile of v1, /device:TPU:2, one launch (start us, length us, event | category | flops | bytes accessed | tf_op | source)
XLA Modules:
  0.0 101.7 jit_solution(9144329081129860789)
XLA Ops:
  1.3 95.2 %layer.1 = bf16[64,2048]{1,0:T(8,128)(2,1)} custom-call(s32[1]{0:T(128)S(6)} %copy.15.length_ref, s32[8,64]{1,0:T(8,128)} %bitcast.28, f32[8,64]{1,0:T(8,128)} %bitcast.29, f32[1,2048]{1,0:T(1,128)} %bitcast.27, bf16[64,2048]{1,0:T(8,128)(2,1)} %bitcast.25, bf16[64,2,2048]{2,1,0:T(2,128)(2,1)} %bitcast.22, bf16[512,2,2048]{2,1,0:T(2,128)(2,1)} %bitcast.16, ...), custom_call_target="tpu_custom_call" | custom-call | tf_op jit(solution)/shard_map/layer/pallas_call | solution.py:316
  96.5 0.0 copy-start
  96.5 4.4 %append.1 = bf16[512,2,2048]{2,1,0:T(2,128)(2,1)} custom-call(s32[1]{0:T(128)S(6)} %copy.15.length_ref, bf16[64,2,2048]{2,1,0:T(2,128)(2,1)} %bitcast.23, bf16[512,2,2048]{2,1,0:T(2,128)(2,1)} %bitcast.17), custom_call_target="tpu_custom_call" | custom-call | tf_op jit(solution)/shard_map/append/pallas_call | solution.py:368
  100.9 0.0 copy-done
  101.0 0.7 copy.16
Async XLA Ops:
  96.5 4.4 %copy-start = (bf16[64,2048]{1,0:T(8,128)(2,1)S(1)}, bf16[64,2048]{1,0:T(8,128)(2,1)}, u32[]{:S(2)}) copy-start(bf16[64,2048]{1,0:T(8,128)(2,1)} %layer.1) | copy-start | bytes 786436

commit v2 on v1

v2 whole, which is shorter than its diff:
```python
import math

import jax
import jax.numpy as jnp
from jax import lax
from jax.experimental import pallas as pl
from jax.experimental.pallas import tpu as pltpu
from jax.sharding import PartitionSpec as P

MESH = pl.DeviceIdType.MESH
F32 = jnp.float32
BF16 = jnp.bfloat16

GROUP = 64
D = 2048
HEADS = 16
HEAD_DIM = 128
EXPERTS = 64
TOP = 8
HALF = 512
CAP = 10
CACHE = 512
SEEN = 448
LANES = 128
PIECES = D // LANES
CHUNKS = 4
PEERS = EXPERTS // CHUNKS
ROWS = PEERS * CAP
MASKED = -1e30 * HEAD_DIM**0.5
AHEAD = 2
GROUPS = 4
STEP = 16
WIDE = D // GROUPS
PAIRS = 2 * (SEEN + GROUP)
SCALE = HEAD_DIM ** (-0.5) / math.log(2.0)


def dot(a, b, dims=((1,), (0,))):
    return lax.dot_general(a, b, (dims, ((), ())), preferred_element_type=F32)


def offsets(i):
    dx, dy = (i // 4) % 4, i % 4
    return (i // PEERS + 8 - dx - dy) % 4, dx, dy


def layer_kernel(
    length_hbm,
    ids_hbm,
    gates_hbm,
    gain_hbm,
    q_hbm,
    keys_ref,
    values_ref,
    res_hbm,
    ow_hbm,
    wg_hbm,
    wu_hbm,
    wd_hbm,
    out_ref,
    length_ref,
    keep_ref,
    ids_ref,
    gates_ref,
    gain_ref,
    q_ref,
    res_ref,
    ow_ref,
    wg_ref,
    wu_ref,
    wd_ref,
    att_ref,
    stream_ref,
    normed_ref,
    pick_ref,
    mixhi_ref,
    mixlo_ref,
    wide_ref,
    x_ref,
    h_ref,
    out_rows,
    in_rows,
    done_rows,
    back_rows,
    local_sem,
    ow_sem,
    mate_send,
    mate_recv,
    send_sem,
    recv_sem,
    back_send,
    back_recv,
):
    z = lax.axis_index("req")
    along = lax.axis_index("exp")
    core = along % 2
    x = along // 8
    y = (along // 2) % 4

    def device(i, sign):
        dz, dx, dy = offsets(i)
        there = (((x + sign * dx + 4) % 4) * 4 + (y + sign * dy + 4) % 4) * 2 + core
        return {"req": (z + sign * dz + 4) % 4, "exp": there}

    mate = {"req": z, "exp": along + 1 - 2 * core}

    small = [
        pltpu.make_async_copy(q_hbm, q_ref, local_sem.at[0]),
        pltpu.make_async_copy(length_hbm, length_ref, local_sem.at[1]),
        pltpu.make_async_copy(res_hbm, res_ref, local_sem.at[2]),
        pltpu.make_async_copy(gain_hbm, gain_ref, local_sem.at[6]),
    ]
    tables = [
        pltpu.make_async_copy(ids_hbm, ids_ref, local_sem.at[7]),
        pltpu.make_async_copy(gates_hbm, gates_ref, local_sem.at[8]),
    ]
    weights = [
        pltpu.make_async_copy(wg_hbm, wg_ref.at[core], local_sem.at[3]),
        pltpu.make_async_copy(wu_hbm, wu_ref.at[core], local_sem.at[4]),
        pltpu.make_async_copy(wd_hbm, wd_ref.at[core], local_sem.at[5]),
    ]

    def ow_copy(g):
        at = pl.ds(pl.multiple_of(g * WIDE, WIDE), WIDE)
        return pltpu.make_async_copy(ow_hbm.at[at], ow_ref.at[at], ow_sem.at[g])

    for copy in tables + small:
        copy.start()

    for g in range(GROUPS):
        ow_copy(g).start()
    barrier = pltpu.get_barrier_semaphore()

    def greet(i, carry):
        pl.semaphore_signal(barrier, inc=1, device_id=device(i, 1), device_id_type=MESH)
        return carry

    lax.fori_loop(1, EXPERTS, greet, 0)
    pl.semaphore_signal(barrier, inc=1, device_id=mate, device_id_type=MESH)

    swaps = [
        pltpu.make_async_remote_copy(
            src_ref=src, dst_ref=dst.at[core], send_sem=mate_send.at[k], recv_sem=mate_recv.at[k],
            device_id=mate, device_id_type=MESH,
        )
        for k, (src, dst) in enumerate(((wg_hbm, wg_ref), (wu_hbm, wu_ref), (wd_hbm, wd_ref)))
    ]

    for copy in tables:
        copy.wait()

    expert_of = lax.broadcasted_iota(jnp.int32, (EXPERTS, GROUP), 0)
    hit = jnp.zeros((EXPERTS, GROUP), F32)
    gate_of = jnp.zeros((EXPERTS, GROUP), F32)
    for k in range(TOP):
        same = ids_ref[k : k + 1, :] == expert_of
        hit = jnp.where(same, 1.0, hit)
        gate_of = jnp.where(same, gates_ref[k : k + 1, :], gate_of)
    t_row = lax.broadcasted_iota(jnp.int32, (GROUP, GROUP), 0)
    t_col = lax.broadcasted_iota(jnp.int32, (GROUP, GROUP), 1)
    before = jnp.where(t_row < t_col, 1.0, 0.0).astype(BF16)
    eye = jnp.where(t_row == t_col, 1.0, 0.0).astype(BF16)
    rank = dot(hit.astype(BF16), before)
    rank = jnp.where(hit > 0.5, rank, 99.0).astype(BF16)
    gate_hi = gate_of.astype(BF16)
    gate_lo = (gate_of - gate_hi.astype(F32)).astype(BF16)

    def slots(shape, axis):
        row = lax.broadcasted_iota(jnp.int32, shape, axis)
        i = (row * 6554) >> 16
        dx, dy = (i >> 2) & 3, i & 3
        dz = ((i >> 4) + 8 - dx - dy) & 3
        expert = (((z + dz) & 3) << 4) + (((x + dx) & 3) << 2) + ((y + dy) & 3)
        return (row - i * CAP).astype(F32), expert

    slot, expert = slots((EXPERTS * CAP, EXPERTS), 0)
    spread = jnp.where(expert == lax.broadcasted_iota(jnp.int32, expert.shape, 1), 1.0, 0.0).astype(BF16)
    pick_ref[...] = jnp.where(dot(spread, rank) == slot, 1.0, 0.0).astype(BF16)
    for copy in small:
        copy.wait()
    place = lax.broadcasted_iota(jnp.int32, (8, SEEN + GROUP), 1)
    length = length_ref[0]
    keep_ref[...] = jnp.where((place < length) | (place >= SEEN), 1.0, 0.0)

    def head(h):
        at = pl.ds(pl.multiple_of(h * HEAD_DIM, HEAD_DIM), HEAD_DIM)
        scores = dot(q_ref[:, at], keys_ref[h], ((1,), (1,)))
        scores = jnp.where(keep_ref[0:1, :] > 0.5, scores, MASKED)
        raised = jnp.exp2((scores - jnp.max(scores, axis=1, keepdims=True)) * SCALE)
        total = jnp.sum(raised, axis=1, keepdims=True)
        att_ref[:, at] = (dot(raised.astype(BF16), values_ref[h]) / total).astype(BF16)

    def group(g, carry):
        heads = [g * (HEADS // GROUPS) + k for k in range(HEADS // GROUPS)]
        for h in heads:
            head(h)
        ow_copy(g).wait()
        at = pl.ds(pl.multiple_of(g * WIDE, WIDE), WIDE)
        for n in range(0, D, 512):
            stream_ref[:, n : n + 512] += dot(att_ref[:, at], ow_ref[at, n : n + 512])
        return carry

    stream_ref[...] = res_ref[...].astype(F32)
    lax.fori_loop(0, 1, group, 0)
    pl.semaphore_wait(barrier, EXPERTS)
    for swap in swaps:
        swap.start()
    lax.fori_loop(1, GROUPS, group, 0)
    for copy in weights:
        copy.start()

    stream = stream_ref[...]
    mean_square = jnp.mean(stream * stream, axis=1, keepdims=True)
    normed_ref[...] = (stream * lax.rsqrt(mean_square + 1e-06) * gain_ref[...]).astype(BF16)

    def send_copy(i):
        return pltpu.make_async_remote_copy(
            src_ref=out_rows.at[i], dst_ref=in_rows.at[i], send_sem=send_sem.at[i], recv_sem=recv_sem.at[i],
            device_id=device(i, 1), device_id_type=MESH,
        )

    def back_copy(i):
        return pltpu.make_async_remote_copy(
            src_ref=done_rows.at[i], dst_ref=back_rows.at[i], send_sem=back_send.at[i], recv_sem=back_recv.at[i],
            device_id=device(i, -1), device_id_type=MESH,
        )

    own_out = pltpu.make_async_copy(out_rows.at[0], in_rows.at[0], recv_sem.at[0])
    own_back = pltpu.make_async_copy(done_rows.at[0], back_rows.at[0], back_recv.at[0])

    def tiles_out(rows, j):
        rows[pl.ds(j * PEERS, PEERS)] = wide_ref[...].reshape(PEERS, CAP, PIECES, LANES).astype(BF16)

    def tiles_in(rows, j):
        wide_ref[...] = rows[pl.ds(j * PEERS, PEERS)].astype(F32).reshape(ROWS * PIECES, LANES)
        for c in range(PIECES):
            x_ref[:, c * LANES : (c + 1) * LANES] = wide_ref[pl.ds(c, ROWS, stride=PIECES), :].astype(BF16)

    def each_peer(j, action):
        def body(i, carry):
            action(i)
            return carry

        lax.fori_loop(j * PEERS + (1 if j == 0 else 0), (j + 1) * PEERS, body, 0)

    def send(j):
        picked = pick_ref[j * ROWS : (j + 1) * ROWS, :]
        for c in range(PIECES):
            wide_ref[pl.ds(c, ROWS, stride=PIECES), :] = dot(picked, normed_ref[:, c * LANES : (c + 1) * LANES])
        tiles_out(out_rows, j)
        if j == 0:
            own_out.start()
        each_peer(j, lambda i: send_copy(i).start())

    for j in range(AHEAD):
        send(j)

    slot, expert = slots((EXPERTS, EXPERTS * CAP), 1)
    spread = jnp.where(expert == lax.broadcasted_iota(jnp.int32, expert.shape, 0), 1.0, 0.0).astype(BF16)
    turned = ((1,), (1,))
    chosen = dot(dot(eye, rank, turned).astype(BF16), spread) == slot
    for table, part in ((mixhi_ref, gate_hi), (mixlo_ref, gate_lo)):
        spread_gate = dot(dot(eye, part, turned).astype(BF16), spread)
        whole = jnp.where(chosen, spread_gate, 0.0).astype(BF16)
        for j in range(CHUNKS):
            table[j] = whole[:, j * ROWS : (j + 1) * ROWS]

    for copy in weights:
        copy.wait()
    for swap in swaps:
        swap.wait()

    for j in range(CHUNKS):
        if j + AHEAD < CHUNKS:
            each_peer(j, lambda i: send_copy(i).wait_send())
            send(j + AHEAD)
        if j == 0:
            own_out.wait()
        each_peer(j, lambda i: send_copy(i).wait_recv())
        tiles_in(in_rows, j)

        def hidden(n, carry):
            half, at = n // 2, pl.ds(pl.multiple_of((n % 2) * 256, 256), 256)
            gate = dot(x_ref[...], wg_ref[half, :, at])
            up = dot(x_ref[...], wu_ref[half, :, at])
            h_ref[:, pl.ds(pl.multiple_of(n * 256, 256), 256)] = (gate / (1.0 + jnp.exp(-gate)) * up).astype(BF16)
            return carry

        lax.fori_loop(0, 4, hidden, 0)

        def down(n, carry):
            at = pl.ds(pl.multiple_of(n * 256, 256), 256)
            rows = dot(h_ref[:, :HALF], wd_ref[0, :, at]) + dot(h_ref[:, HALF:], wd_ref[1, :, at])
            wide_ref[pl.ds(2 * n, ROWS, stride=PIECES), :] = rows[:, :LANES]
            wide_ref[pl.ds(2 * n + 1, ROWS, stride=PIECES), :] = rows[:, LANES:]
            return carry

        lax.fori_loop(0, D // 256, down, 0, unroll=2)
        tiles_out(done_rows, j)
        if j == 0:
            own_back.start()
        each_peer(j, lambda i: back_copy(i).start())

    for j in range(CHUNKS):
        if j == 0:
            own_back.wait()
        each_peer(j, lambda i: back_copy(i).wait_recv())
        tiles_in(back_rows, j)
        for n in range(D // 512):
            at = slice(n * 512, (n + 1) * 512)
            stream_ref[:, at] += dot(mixhi_ref[j], x_ref[:, at]) + dot(mixlo_ref[j], x_ref[:, at])
    out_ref[...] = stream_ref[...].astype(BF16)

    for j in range(CHUNKS):
        if j + AHEAD >= CHUNKS:
            each_peer(j, lambda i: send_copy(i).wait_send())
        each_peer(j, lambda i: back_copy(i).wait_send())


def append_kernel(
    length_hbm, kv_hbm, cache_hbm, out_hbm, keys_ref, values_ref, length_ref, held, new, flat_ref, in_sem, out_sem
):
    fetch = pltpu.make_async_copy(kv_hbm, new, in_sem.at[GROUPS + 1])
    place = pltpu.make_async_copy(length_hbm, length_ref, in_sem.at[GROUPS + 2])

    def moves(g):
        at = pl.ds(pl.multiple_of(g * WIDE, WIDE), WIDE)
        arrive = pltpu.make_async_copy(cache_hbm.at[:, :, at], held.at[:, :, at], in_sem.at[g])
        leave = pltpu.make_async_copy(held.at[:, :, at], out_hbm.at[:, :, at], out_sem.at[g])
        return arrive, leave

    place.start()
    fetch.start()
    for g in range(GROUPS):
        moves(g)[0].start()
    fetch.wait()
    place.wait()

    def group(g, carry):
        arrive, leave = moves(g)
        arrive.wait()
        leave.start()
        for k in range(HEADS // GROUPS):
            turn(g * (HEADS // GROUPS) + k, k)
        return carry

    def turn(h, k):
        at = pl.ds(pl.multiple_of(h * HEAD_DIM, HEAD_DIM), HEAD_DIM)
        flat = flat_ref.at[k]
        for p in range(0, SEEN, STEP):
            flat[2 * p : 2 * (p + STEP), :] = held[p : p + STEP, :, at].reshape(2 * STEP, HEAD_DIM).astype(F32)
        flat[2 * SEEN : PAIRS, :] = new[:, :, at].reshape(2 * GROUP, HEAD_DIM).astype(F32)
        keys_ref[h] = flat[pl.ds(0, SEEN + GROUP, stride=2), :].astype(BF16)
        values_ref[h] = flat[pl.ds(1, SEEN + GROUP, stride=2), :].astype(BF16)

    lax.fori_loop(0, GROUPS, group, 0)
    for g in range(GROUPS):
        moves(g)[1].wait()
    write = pltpu.make_async_copy(new, out_hbm.at[pl.ds(length_ref[0], GROUP)], out_sem.at[GROUPS])
    write.start()
    write.wait()


def shards(
    queries, new_kv, cache, lengths, residual, out_weight, norm_gain, expert_ids, gates, w_gate, w_up, w_down
):
    anywhere = pl.BlockSpec(memory_space=pl.ANY)
    in_vmem = pl.BlockSpec(memory_space=pltpu.VMEM)
    tiles = (EXPERTS, CAP, PIECES, LANES)
    appended, keys, values = pl.pallas_call(
        append_kernel,
        name="append",
        out_shape=(
            jax.ShapeDtypeStruct((CACHE, 2, D), BF16),
            pltpu.VMEM((HEADS, SEEN + GROUP, HEAD_DIM), BF16),
            pltpu.VMEM((HEADS, SEEN + GROUP, HEAD_DIM), BF16),
        ),
        in_specs=[anywhere, anywhere, anywhere],
        out_specs=(anywhere, in_vmem, in_vmem),
        scratch_shapes=[
            pltpu.SMEM((1,), jnp.int32),
            pltpu.VMEM((CACHE, 2, D), BF16),
            pltpu.VMEM((GROUP, 2, D), BF16),
            pltpu.VMEM((HEADS // GROUPS, PAIRS, HEAD_DIM), F32),
            pltpu.SemaphoreType.DMA((GROUPS + 3,)),
            pltpu.SemaphoreType.DMA((GROUPS + 1,)),
        ],
        compiler_params=pltpu.CompilerParams(vmem_limit_bytes=58 * 1024 * 1024),
    )(lengths, new_kv[0], cache[0])
    layer_out = pl.pallas_call(
        layer_kernel,
        name="layer",
        out_shape=pltpu.VMEM((GROUP, D), BF16),
        in_specs=[anywhere] * 5 + [in_vmem, in_vmem] + [anywhere] * 5,
        out_specs=in_vmem,
        scratch_shapes=[
            pltpu.SMEM((1,), jnp.int32),
            pltpu.VMEM((8, SEEN + GROUP), F32),
            pltpu.VMEM((TOP, GROUP), jnp.int32),
            pltpu.VMEM((TOP, GROUP), F32),
            pltpu.VMEM((1, D), F32),
            pltpu.VMEM((GROUP, D), BF16),
            pltpu.VMEM((GROUP, D), BF16),
            pltpu.VMEM((D, D), BF16),
            pltpu.VMEM((2, D, HALF), BF16),
            pltpu.VMEM((2, D, HALF), BF16),
            pltpu.VMEM((2, HALF, D), BF16),
            pltpu.VMEM((GROUP, D), BF16),
            pltpu.VMEM((GROUP, D), F32),
            pltpu.VMEM((GROUP, D), BF16),
            pltpu.VMEM((EXPERTS * CAP, GROUP), BF16),
            pltpu.VMEM((CHUNKS, GROUP, ROWS), BF16),
            pltpu.VMEM((CHUNKS, GROUP, ROWS), BF16),
            pltpu.VMEM((ROWS * PIECES, LANES), F32),
            pltpu.VMEM((ROWS, D), BF16),
            pltpu.VMEM((ROWS, 2 * HALF), BF16),
            pltpu.VMEM(tiles, BF16),
            pltpu.VMEM(tiles, BF16),
            pltpu.VMEM(tiles, BF16),
            pltpu.VMEM(tiles, BF16),
            pltpu.SemaphoreType.DMA((9,)),
            pltpu.SemaphoreType.DMA((GROUPS,)),
            pltpu.SemaphoreType.DMA((3,)),
            pltpu.SemaphoreType.DMA((3,)),
            pltpu.SemaphoreType.DMA((EXPERTS,)),
            pltpu.SemaphoreType.DMA((EXPERTS,)),
            pltpu.SemaphoreType.DMA((EXPERTS,)),
            pltpu.SemaphoreType.DMA((EXPERTS,)),
        ],
        compiler_params=pltpu.CompilerParams(
            collective_id=0, has_side_effects=True, vmem_limit_bytes=58 * 1024 * 1024
        ),
    )(
        lengths,
        expert_ids[0].T,
        gates[0].T,
        norm_gain[None],
        queries[0],
        pltpu.with_memory_space_constraint(keys, pltpu.VMEM),
        pltpu.with_memory_space_constraint(values, pltpu.VMEM),
        residual[0],
        out_weight,
        w_gate[0],
        w_up[0],
        w_down[0],
    )
    return layer_out[None], appended[None]


def solution(mesh):
    shared = ("req", "exp")
    three, four = P(shared, None, None), P(shared, None, None, None)
    return jax.shard_map(
        shards,
        mesh=mesh,
        in_specs=(three, four, four, P(shared), three, P(), P(), three, three, three, three, three),
        out_specs=(three, four),
        check_vma=False,
    )
```

time: 103 us -> 89.9 us (0.87)
  Pallas kernels: 99.6 us -> 86.5 us
    pallas_call x2, Pallas kernels: 99.6 us -> 86.5 us  [the longest x1 80.8 us: shards(): pl.pallas_call(layer_kernel, name='layer', out_shape=pltpu.VMEM((GROUP, D...]
where the time goes in v2:
time: 89.9 us; the launch traced here: 88.5 us
  Pallas kernels  86.5 us (96%)
  between operations  1.29 us (1%)
    pallas_call x1, Pallas kernels, shards(): pl.pallas_call(layer_kernel, name='layer', out_shape=pltpu.VMEM((GROUP, D...  80.8 us
    pallas_call x1, Pallas kernels, shards(): pl.pallas_call(append_kernel, name='append', out_shape=(jax.ShapeDtypeStr...  5.7 us

profile of v2, /device:TPU:2, one launch (start us, length us, event | category | flops | bytes accessed | tf_op | source)
XLA Modules:
  0.0 88.5 jit_solution(1181624836165190003)
XLA Ops:
  1.3 5.7 %append.1 = (bf16[512,2,2048]{2,1,0:T(2,128)(2,1)}, bf16[16,512,128]{2,1,0:T(8,128)(2,1)S(1)}, bf16[16,512,128]{2,1,0:T(8,128)(2,1)S(1)}) custom-call(s32[1]{0:T(128)S(6)} %copy.16.length_hbm, bf16[64,2,2048]{2,1,0:T(2,128)(2,1)} %bitcast.21, bf16[512,2,2048]{2,1,0:T(2,128)(2,1)} %bitcast.17), custom_call_target="tpu_custom_call" | custom-call | tf_op jit(solution)/shard_map/append/pallas_call | solution.py:370
  7.0 80.8 %layer.1 = bf16[64,2048]{1,0:T(8,128)(2,1)S(1)} custom-call(s32[1]{0:T(128)S(6)} %copy.16.length_hbm, s32[8,64]{1,0:T(8,128)} %bitcast.25, f32[8,64]{1,0:T(8,128)} %bitcast.26, f32[1,2048]{1,0:T(1,128)} %bitcast.24, bf16[64,2048]{1,0:T(8,128)(2,1)} %bitcast.22, bf16[16,512,128]{2,1,0:T(8,128)(2,1)S(1)} %get-tuple-element.5.keys_ref, ...), custom_call_target="tpu_custom_call" | custom-call | tf_op jit(solution)/shard_map/layer/pallas_call | solution.py:390
  87.8 0.7 copy.15

commit v3 on v2

--- a/solution.py
+++ b/solution.py
@@ -97,10 +97,13 @@
     x = along // 8
     y = (along // 2) % 4
 
+    zs = [lax.rem(z + d, 4) for d in range(4)]
+    xs = [lax.rem(x + d, 4) * 8 for d in range(4)]
+    ys = [lax.rem(y + d, 4) * 2 + core for d in range(4)]
+
     def device(i, sign):
-        dz, dx, dy = offsets(i)
-        there = (((x + sign * dx + 4) % 4) * 4 + (y + sign * dy + 4) % 4) * 2 + core
-        return {"req": (z + sign * dz + 4) % 4, "exp": there}
+        dz, dx, dy = (sign * d % 4 for d in offsets(i))
+        return {"req": zs[dz], "exp": xs[dx] + ys[dy]}
 
     mate = {"req": z, "exp": along + 1 - 2 * core}
 
@@ -131,11 +134,8 @@
         ow_copy(g).start()
     barrier = pltpu.get_barrier_semaphore()
 
-    def greet(i, carry):
+    for i in range(1, EXPERTS):
         pl.semaphore_signal(barrier, inc=1, device_id=device(i, 1), device_id_type=MESH)
-        return carry
-
-    lax.fori_loop(1, EXPERTS, greet, 0)
     pl.semaphore_signal(barrier, inc=1, device_id=mate, device_id_type=MESH)
 
     swaps = [
@@ -213,20 +213,31 @@
     mean_square = jnp.mean(stream * stream, axis=1, keepdims=True)
     normed_ref[...] = (stream * lax.rsqrt(mean_square + 1e-06) * gain_ref[...]).astype(BF16)
 
-    def send_copy(i):
+    def send_copy(j, part, peer):
         return pltpu.make_async_remote_copy(
-            src_ref=out_rows.at[i], dst_ref=in_rows.at[i], send_sem=send_sem.at[i], recv_sem=recv_sem.at[i],
-            device_id=device(i, 1), device_id_type=MESH,
+            src_ref=out_rows.at[part], dst_ref=in_rows.at[part], send_sem=send_sem.at[j], recv_sem=recv_sem.at[j],
+            device_id=peer, device_id_type=MESH,
         )
 
-    def back_copy(i):
+    def back_copy(j, part, peer):
         return pltpu.make_async_remote_copy(
-            src_ref=done_rows.at[i], dst_ref=back_rows.at[i], send_sem=back_send.at[i], recv_sem=back_recv.at[i],
-            device_id=device(i, -1), device_id_type=MESH,
+            src_ref=done_rows.at[part], dst_ref=back_rows.at[part], send_sem=back_send.at[j],
+            recv_sem=back_recv.at[j], device_id=peer, device_id_type=MESH,
         )
 
-    own_out = pltpu.make_async_copy(out_rows.at[0], in_rows.at[0], recv_sem.at[0])
-    own_back = pltpu.make_async_copy(done_rows.at[0], back_rows.at[0], back_recv.at[0])
+    def start_chunk(copy, j, sign):
+        for i in range(max(j * PEERS, 1), (j + 1) * PEERS):
+            copy(j, pl.ds(i, 1), device(i, sign)).start()
+
+    def chunk_sent(copy, j):
+        first = max(j * PEERS, 1)
+        copy(j, pl.ds(first, (j + 1) * PEERS - first), mate).wait_send()
+
+    def chunk_here(copy, j):
+        copy(j, pl.ds(j * PEERS, PEERS), mate).wait_recv()
+
+    own_out = pltpu.make_async_copy(out_rows.at[pl.ds(0, 1)], in_rows.at[pl.ds(0, 1)], recv_sem.at[0])
+    own_back = pltpu.make_async_copy(done_rows.at[pl.ds(0, 1)], back_rows.at[pl.ds(0, 1)], back_recv.at[0])
 
     def tiles_out(rows, j):
         rows[pl.ds(j * PEERS, PEERS)] = wide_ref[...].reshape(PEERS, CAP, PIECES, LANES).astype(BF16)
@@ -235,13 +246,6 @@
         wide_ref[...] = rows[pl.ds(j * PEERS, PEERS)].astype(F32).reshape(ROWS * PIECES, LANES)
         for c in range(PIECES):
             x_ref[:, c * LANES : (c + 1) * LANES] = wide_ref[pl.ds(c, ROWS, stride=PIECES), :].astype(BF16)
-
-    def each_peer(j, action):
-        def body(i, carry):
-            action(i)
-            return carry
-
-        lax.fori_loop(j * PEERS + (1 if j == 0 else 0), (j + 1) * PEERS, body, 0)
 
     def send(j):
         picked = pick_ref[j * ROWS : (j + 1) * ROWS, :]
@@ -250,7 +254,7 @@
         tiles_out(out_rows, j)
         if j == 0:
             own_out.start()
-        each_peer(j, lambda i: send_copy(i).start())
+        start_chunk(send_copy, j, 1)
 
     for j in range(AHEAD):
         send(j)
@@ -272,11 +276,9 @@
 
     for j in range(CHUNKS):
         if j + AHEAD < CHUNKS:
-            each_peer(j, lambda i: send_copy(i).wait_send())
+            chunk_sent(send_copy, j)
             send(j + AHEAD)
-        if j == 0:
-            own_out.wait()
-        each_peer(j, lambda i: send_copy(i).wait_recv())
+        chunk_here(send_copy, j)
         tiles_in(in_rows, j)
 
         def hidden(n, carry):
@@ -299,12 +301,10 @@
         tiles_out(done_rows, j)
         if j == 0:
             own_back.start()
-        each_peer(j, lambda i: back_copy(i).start())
+        start_chunk(back_copy, j, -1)
 
     for j in range(CHUNKS):
-        if j == 0:
-            own_back.wait()
-        each_peer(j, lambda i: back_copy(i).wait_recv())
+        chunk_here(back_copy, j)
         tiles_in(back_rows, j)
         for n in range(D // 512):
             at = slice(n * 512, (n + 1) * 512)
@@ -313,8 +313,8 @@
 
     for j in range(CHUNKS):
         if j + AHEAD >= CHUNKS:
-            each_peer(j, lambda i: send_copy(i).wait_send())
-        each_peer(j, lambda i: back_copy(i).wait_send())
+            chunk_sent(send_copy, j)
+        chunk_sent(back_copy, j)
 
 
 def append_kernel(
@@ -422,10 +422,10 @@
             pltpu.SemaphoreType.DMA((GROUPS,)),
             pltpu.SemaphoreType.DMA((3,)),
             pltpu.SemaphoreType.DMA((3,)),
-            pltpu.SemaphoreType.DMA((EXPERTS,)),
-            pltpu.SemaphoreType.DMA((EXPERTS,)),
-            pltpu.SemaphoreType.DMA((EXPERTS,)),
-            pltpu.SemaphoreType.DMA((EXPERTS,)),
+            pltpu.SemaphoreType.DMA((CHUNKS,)),
+            pltpu.SemaphoreType.DMA((CHUNKS,)),
+            pltpu.SemaphoreType.DMA((CHUNKS,)),
+            pltpu.SemaphoreType.DMA((CHUNKS,)),
         ],
         compiler_params=pltpu.CompilerParams(
             collective_id=0, has_side_effects=True, vmem_limit_bytes=58 * 1024 * 1024

time: 89.9 us -> 95.7 us (1.065); the launches traced: 88.5 us -> 95.6 us
  Pallas kernels: 86.5 us -> 93.6 us
    pallas_call x1, Pallas kernels: 80.8 us -> 87.9 us  [shards(): pl.pallas_call(layer_kernel, name='layer', out_shape=pltpu.VMEM((GROUP, D...]
where the time goes in v3:
time: 95.7 us; the launch traced here: 95.6 us
  Pallas kernels  93.6 us (98%)
  between operations  1.29 us (1%)
    pallas_call x1, Pallas kernels, shards(): pl.pallas_call(layer_kernel, name='layer', out_shape=pltpu.VMEM((GROUP, D...  87.9 us
    pallas_call x1, Pallas kernels, shards(): pl.pallas_call(append_kernel, name='append', out_shape=(jax.ShapeDtypeStr...  5.7 us

profile of v3, /device:TPU:2, one launch (start us, length us, event | category | flops | bytes accessed | tf_op | source)
XLA Modules:
  0.0 95.6 jit_solution(777140448795450029)
XLA Ops:
  1.3 5.7 %append.1 = (bf16[512,2,2048]{2,1,0:T(2,128)(2,1)}, bf16[16,512,128]{2,1,0:T(8,128)(2,1)S(1)}, bf16[16,512,128]{2,1,0:T(8,128)(2,1)S(1)}) custom-call(s32[1]{0:T(128)S(6)} %copy.16.length_hbm, bf16[64,2,2048]{2,1,0:T(2,128)(2,1)} %bitcast.21, bf16[512,2,2048]{2,1,0:T(2,128)(2,1)} %bitcast.17), custom_call_target="tpu_custom_call" | custom-call | tf_op jit(solution)/shard_map/append/pallas_call | solution.py:370
  7.0 87.9 %layer.1 = bf16[64,2048]{1,0:T(8,128)(2,1)S(1)} custom-call(s32[1]{0:T(128)S(6)} %copy.16.length_hbm, s32[8,64]{1,0:T(8,128)} %bitcast.25, f32[8,64]{1,0:T(8,128)} %bitcast.26, f32[1,2048]{1,0:T(1,128)} %bitcast.24, bf16[64,2048]{1,0:T(8,128)(2,1)} %bitcast.22, bf16[16,512,128]{2,1,0:T(8,128)(2,1)S(1)} %get-tuple-element.5.keys_ref, ...), custom_call_target="tpu_custom_call" | custom-call | tf_op jit(solution)/shard_map/layer/pallas_call | solution.py:390
  94.9 0.7 copy.15

commit v4 on v2

--- a/solution.py
+++ b/solution.py
@@ -213,16 +213,16 @@
     mean_square = jnp.mean(stream * stream, axis=1, keepdims=True)
     normed_ref[...] = (stream * lax.rsqrt(mean_square + 1e-06) * gain_ref[...]).astype(BF16)
 
-    def send_copy(i):
+    def send_copy(i, peer=None):
         return pltpu.make_async_remote_copy(
             src_ref=out_rows.at[i], dst_ref=in_rows.at[i], send_sem=send_sem.at[i], recv_sem=recv_sem.at[i],
-            device_id=device(i, 1), device_id_type=MESH,
+            device_id=peer or device(i, 1), device_id_type=MESH,
         )
 
-    def back_copy(i):
+    def back_copy(i, peer=None):
         return pltpu.make_async_remote_copy(
             src_ref=done_rows.at[i], dst_ref=back_rows.at[i], send_sem=back_send.at[i], recv_sem=back_recv.at[i],
-            device_id=device(i, -1), device_id_type=MESH,
+            device_id=peer or device(i, -1), device_id_type=MESH,
         )
 
     own_out = pltpu.make_async_copy(out_rows.at[0], in_rows.at[0], recv_sem.at[0])
@@ -311,10 +311,10 @@
             stream_ref[:, at] += dot(mixhi_ref[j], x_ref[:, at]) + dot(mixlo_ref[j], x_ref[:, at])
     out_ref[...] = stream_ref[...].astype(BF16)
 
-    for j in range(CHUNKS):
-        if j + AHEAD >= CHUNKS:
-            each_peer(j, lambda i: send_copy(i).wait_send())
-        each_peer(j, lambda i: back_copy(i).wait_send())
+    for i in range((CHUNKS - AHEAD) * PEERS, EXPERTS):
+        send_copy(i, mate).wait_send()
+    for i in range(1, EXPERTS):
+        back_copy(i, mate).wait_send()
 
 
 def append_kernel(

time: 89.9 us -> 89.4 us (level)
  no operation moved by 1% of the time
where the time goes in v4:
time: 89.4 us; the launch traced here: 88.1 us
  Pallas kernels  86.1 us (96%)
  between operations  1.29 us (1%)
    pallas_call x1, Pallas kernels, shards(): pl.pallas_call(layer_kernel, name='layer', out_shape=pltpu.VMEM((GROUP, D...  80.4 us
    pallas_call x1, Pallas kernels, shards(): pl.pallas_call(append_kernel, name='append', out_shape=(jax.ShapeDtypeStr...  5.7 us

profile of v4, /device:TPU:2, one launch (start us, length us, event | category | flops | bytes accessed | tf_op | source)
XLA Modules:
  0.0 88.1 jit_solution(15726487980843370291)
XLA Ops:
  1.3 5.7 %append.1 = (bf16[512,2,2048]{2,1,0:T(2,128)(2,1)}, bf16[16,512,128]{2,1,0:T(8,128)(2,1)S(1)}, bf16[16,512,128]{2,1,0:T(8,128)(2,1)S(1)}) custom-call(s32[1]{0:T(128)S(6)} %copy.16.length_hbm, bf16[64,2,2048]{2,1,0:T(2,128)(2,1)} %bitcast.21, bf16[512,2,2048]{2,1,0:T(2,128)(2,1)} %bitcast.17), custom_call_target="tpu_custom_call" | custom-call | tf_op jit(solution)/shard_map/append/pallas_call | solution.py:370
  7.0 80.4 %layer.1 = bf16[64,2048]{1,0:T(8,128)(2,1)S(1)} custom-call(s32[1]{0:T(128)S(6)} %copy.16.length_hbm, s32[8,64]{1,0:T(8,128)} %bitcast.25, f32[8,64]{1,0:T(8,128)} %bitcast.26, f32[1,2048]{1,0:T(1,128)} %bitcast.24, bf16[64,2048]{1,0:T(8,128)(2,1)} %bitcast.22, bf16[16,512,128]{2,1,0:T(8,128)(2,1)S(1)} %get-tuple-element.5.keys_ref, ...), custom_call_target="tpu_custom_call" | custom-call | tf_op jit(solution)/shard_map/layer/pallas_call | solution.py:390
  87.4 0.7 copy.15

commit v5 on v4

--- a/solution.py
+++ b/solution.py
@@ -25,6 +25,7 @@
 PIECES = D // LANES
 CHUNKS = 4
 PEERS = EXPERTS // CHUNKS
+BATCH = 8
 ROWS = PEERS * CAP
 MASKED = -1e30 * HEAD_DIM**0.5
 AHEAD = 2
@@ -76,6 +77,8 @@
     mixhi_ref,
     mixlo_ref,
     wide_ref,
+    wide_even,
+    wide_odd,
     x_ref,
     h_ref,
     out_rows,
@@ -228,13 +231,20 @@
     own_out = pltpu.make_async_copy(out_rows.at[0], in_rows.at[0], recv_sem.at[0])
     own_back = pltpu.make_async_copy(done_rows.at[0], back_rows.at[0], back_recv.at[0])
 
+    wide_refs = (wide_even, wide_odd)
+
     def tiles_out(rows, j):
         rows[pl.ds(j * PEERS, PEERS)] = wide_ref[...].reshape(PEERS, CAP, PIECES, LANES).astype(BF16)
 
     def tiles_in(rows, j):
-        wide_ref[...] = rows[pl.ds(j * PEERS, PEERS)].astype(F32).reshape(ROWS * PIECES, LANES)
-        for c in range(PIECES):
-            x_ref[:, c * LANES : (c + 1) * LANES] = wide_ref[pl.ds(c, ROWS, stride=PIECES), :].astype(BF16)
+        for k in range(0, PEERS, BATCH):
+            wide = wide_refs[k // BATCH % 2]
+            size = BATCH * CAP
+            wide[...] = rows[pl.ds(j * PEERS + k, BATCH)].astype(F32).reshape(size * PIECES, LANES)
+            for c in range(PIECES):
+                x_ref[k * CAP : k * CAP + size, c * LANES : (c + 1) * LANES] = wide[
+                    pl.ds(c, size, stride=PIECES), :
+                ].astype(BF16)
 
     def each_peer(j, action):
         def body(i, carry):
@@ -412,6 +422,8 @@
             pltpu.VMEM((CHUNKS, GROUP, ROWS), BF16),
             pltpu.VMEM((CHUNKS, GROUP, ROWS), BF16),
             pltpu.VMEM((ROWS * PIECES, LANES), F32),
+            pltpu.VMEM((BATCH * CAP * PIECES, LANES), F32),
+            pltpu.VMEM((BATCH * CAP * PIECES, LANES), F32),
             pltpu.VMEM((ROWS, D), BF16),
             pltpu.VMEM((ROWS, 2 * HALF), BF16),
             pltpu.VMEM(tiles, BF16),

time: 89.4 us -> 89.4 us (level)
  no operation moved by 1% of the time
where the time goes in v5:
time: 89.4 us; the launch traced here: 88.1 us
  Pallas kernels  86.1 us (96%)
  between operations  1.29 us (1%)
    pallas_call x1, Pallas kernels, shards(): pl.pallas_call(layer_kernel, name='layer', out_shape=pltpu.VMEM((GROUP, D...  80.4 us
    pallas_call x1, Pallas kernels, shards(): pl.pallas_call(append_kernel, name='append', out_shape=(jax.ShapeDtypeStr...  5.7 us

profile of v5, /device:TPU:2, one launch (start us, length us, event | category | flops | bytes accessed | tf_op | source)
XLA Modules:
  0.0 88.1 jit_solution(12501061398725804291)
XLA Ops:
  1.3 5.7 %append.1 = (bf16[512,2,2048]{2,1,0:T(2,128)(2,1)}, bf16[16,512,128]{2,1,0:T(8,128)(2,1)S(1)}, bf16[16,512,128]{2,1,0:T(8,128)(2,1)S(1)}) custom-call(s32[1]{0:T(128)S(6)} %copy.16.length_hbm, bf16[64,2,2048]{2,1,0:T(2,128)(2,1)} %bitcast.21, bf16[512,2,2048]{2,1,0:T(2,128)(2,1)} %bitcast.17), custom_call_target="tpu_custom_call" | custom-call | tf_op jit(solution)/shard_map/append/pallas_call | solution.py:380
  7.0 80.4 %layer.1 = bf16[64,2048]{1,0:T(8,128)(2,1)S(1)} custom-call(s32[1]{0:T(128)S(6)} %copy.16.length_hbm, s32[8,64]{1,0:T(8,128)} %bitcast.25, f32[8,64]{1,0:T(8,128)} %bitcast.26, f32[1,2048]{1,0:T(1,128)} %bitcast.24, bf16[64,2048]{1,0:T(8,128)(2,1)} %bitcast.22, bf16[16,512,128]{2,1,0:T(8,128)(2,1)S(1)} %get-tuple-element.5.keys_ref, ...), custom_call_target="tpu_custom_call" | custom-call | tf_op jit(solution)/shard_map/layer/pallas_call | solution.py:400
  87.4 0.7 copy.15
